TPU v7x, 256 devices: a whole 4x4x8 slice. The times are simulated.
256 devices in a mesh: frame: 16 (over z_lo, x), strip: 16 (over z_hi, y, core).
Axes of the slice: x: 4, y: 4, z: 8 (z_hi: 2, z_lo: 4; z = z_hi * 4 + z_lo), core: 2. Of those that a mesh axis runs over, the one named last changes fastest.
Arguments:
- movie: bfloat16 [128, 1024, 2048], P('frame', 'strip'), may hold values from -17 to 22, as said below
Outputs:
- lag_maps: float32 [25, 1024, 2048], P(None, 'strip', 'frame')
Inputs may be any that keep to these rules, and one draw needn't show every extreme that they name: Frames of a camera movie.
All inputs are finite; a program needn't handle non-finite values.
Results may differ from a plain program's by a relative error of at most 0.0004.
Values may be sent and summed in bfloat16 or wider, within the bound.
A program may use at most 64 MiB of HBM per device.

v0:
```python
import jax
import jax.numpy as jnp
from jax import lax
from jax.sharding import PartitionSpec as P


def padded_2(value, sides, width):
    for axis, dim in sides:
        peers, length = (lax.axis_size(axis), value.shape[dim])
        up = [(i, (i + 1) % peers) for i in range(peers - 1)]
        down = [(j, i) for i, j in up]
        last = lax.slice_in_dim(value, length - width, length, axis=dim)
        initial = lax.slice_in_dim(value, 0, width, axis=dim)
        before = lax.ppermute(last, axis, up)
        after = lax.ppermute(initial, axis, down)
        value = jnp.concatenate([before, value, after], axis=dim)
    return value


def lag_products(field, rows, columns):
    centre = field[:, 2 : 2 + rows, 2 : 2 + columns]
    products = []
    for row_lag in range(-2, 3):
        for col_lag in range(-2, 3):
            shifted = field[
                :, 2 + row_lag : 2 + row_lag + rows, 2 + col_lag : 2 + col_lag + columns
            ]
            products.append(jnp.sum(centre * shifted, axis=0))
    return jnp.stack(products)


def pad_columns(field):
    return jnp.pad(field, ((0, 0), (0, 0), (2, 2)))


def body(movie):
    frames_here, rows, width = movie.shape
    frame_count = lax.axis_size("frame")
    frames_total = frames_here * frame_count
    padded = padded_2(movie, (("strip", 1),), 2)
    raw_values = padded.astype(jnp.float32)
    pixel_mean = (
        lax.psum(jnp.sum(raw_values, axis=0).astype(jnp.bfloat16), "frame").astype(jnp.float32)
        / frames_total
    )
    fluctuation = pad_columns(raw_values - pixel_mean)
    lag_share = lax.psum_scatter(
        lag_products(fluctuation, rows, width), "frame", scatter_dimension=2, tiled=True
    )
    return lag_share / frames_total


def solution(mesh):
    return jax.shard_map(
        body,
        mesh=mesh,
        in_specs=(P("frame", "strip", None),),
        out_specs=P(None, "strip", "frame"),
        check_vma=False,
    )
```

profile of v0, /device:TPU:1, one launch (start us, length us, event | category | flops | bytes accessed | tf_op | source)
XLA Modules:
  0.0 431.6 jit_solution(7262845705202753640)
XLA Ops:
  6.5 1.3 fusion.5
  7.8 4.6 %collective-permute-start = (bf16[8,2,2048]{2,1,0:T(2,128)(2,1)S(1)}, bf16[8,2,2048]{2,1,0:T(2,128)(2,1)S(1)}, u32[]{:S(2)}, u32[]{:S(2)}) collective-permute-start(bf16[8,2,2048]{2,1,0:T(2,128)(2,1)S(1)} %get-tuple-element.36), channel_id=1, source_target_pairs={{0,1},{1,2},{2,3},{3,4},{4,5},{5,6},{6,7},{7,8},{8,9},{9,10},{10,1... | collective-permute-start | bytes 196616 | tf_op jit(solution)/shard_map/ppermute | solution.py:14
  12.4 1.9 collective-permute-start.1
  14.4 3.6 collective-permute-done.1
  18.0 3.1 fusion.4
  21.2 153.5 %all-reduce.3.cloned.1.call-done = bf16[68,2048]{1,0:T(8,128)(2,1)} async-done(((bf16[68,2048]{1,0:T(8,128)(2,1)}), bf16[68,2048]{1,0:T(8,128)(2,1)}) %all-reduce.3.cloned.1.call-update) | async-done | bytes 278544 | tf_op jit(solution)/shard_map/psum | solution.py:43
  174.7 1.0 convert_multiply_fusion
  175.7 0.9 convert_subtract_fusion
  176.6 2.1 copy-done
  178.7 13.1 %multiply_reduce_fusion = (f32[64,2048]{1,0:T(8,128)}, f32[64,2048]{1,0:T(8,128)}, f32[64,2048]{1,0:T(8,128)}, f32[64,2048]{1,0:T(8,128)}, f32[64,2048]{1,0:T(8,...) fusion(f32[8,68,2048]{2,1,0:T(8,128)S(1)} %convert_subtract_fusion), kind=kLoop, calls=%fused_computation.9 | loop fusion | flops 19660800 | bytes 14155776 | tf_op jit(solution)/shard_map/reduce_sum | solution.py:28
  191.8 45.1 %multiply_reduce_fusion.1 = (f32[64,2048]{1,0:T(8,128)S(1)}, f32[64,2048]{1,0:T(8,128)}, f32[64,2048]{1,0:T(8,128)}, f32[64,2048]{1,0:T(8,128)}, f32[64,2048]{1,...) fusion(f32[8,68,2048]{2,1,0:T(8,128)} %copy-done), kind=kLoop, calls=%fused_computation.10 | loop fusion | flops 29491200 | bytes 33554432 | tf_op jit(solution)/shard_map/reduce_sum | solution.py:28
  236.9 2.0 bitcast_dynamic-update-slice_fusion.24
  238.9 1.9 bitcast_dynamic-update-slice_fusion.23
  240.9 2.0 bitcast_dynamic-update-slice_fusion.22
  242.8 1.9 bitcast_dynamic-update-slice_fusion.21
  244.8 1.9 bitcast_dynamic-update-slice_fusion.20
  246.7 0.8 bitcast_dynamic-update-slice_fusion.19
  248.4 0.8 bitcast_dynamic-update-slice_fusion.17
  250.1 0.9 bitcast_dynamic-update-slice_fusion.15
  250.9 0.8 bitcast_dynamic-update-slice_fusion.14
  251.8 0.8 bitcast_dynamic-update-slice_fusion.13
  252.6 0.8 bitcast_dynamic-update-slice_fusion.12
  253.5 0.9 bitcast_dynamic-update-slice_fusion.11
  255.2 0.8 bitcast_dynamic-update-slice_fusion.9
  256.0 0.9 bitcast_dynamic-update-slice_fusion.8
  256.9 0.9 bitcast_dynamic-update-slice_fusion.7
  259.5 0.9 bitcast_dynamic-update-slice_fusion.4
  260.3 0.8 bitcast_dynamic-update-slice_fusion.3
  262.0 0.8 bitcast_dynamic-update-slice_fusion.1
  262.9 0.9 bitcast_dynamic-update-slice_fusion
  263.7 158.9 %reduce-scatter.2.cloned.1.call-done = f32[25,64,128]{2,1,0:T(8,128)} async-done(((f32[25,64,2048]{2,1,0:T(8,128)}), f32[25,64,128]{2,1,0:T(8,128)}) %reduce-scatter.2.cloned.1.call-update) | async-done | bytes 819216 | tf_op jit(solution)/shard_map/reduce_scatter | solution.py:47
  422.6 2.1 broadcast_multiply_fusion
  (42 shorter events, 5.1 us)
Async XLA Ops:
  6.5 169.2 %copy-start.1 = (bf16[8,64,2048]{2,1,0:T(8,128)(2,1)S(1)}, bf16[8,64,2048]{2,1,0:T(8,128)(2,1)}, u32[]{:S(2)}) copy-start(bf16[8,64,2048]{2,1,0:T(8,128)(2,1)} %param.1) | copy-start | bytes 6291460
  6.5 168.1 %all-reduce.3.cloned.1.call-start = ((), (), s32[]{:S(2)}) async-start(), calls=%async_computation.1 | async-start | bytes 589824 | tf_op jit(solution)/shard_map/psum | solution.py:43
  7.8 6.5 %collective-permute-start = (bf16[8,2,2048]{2,1,0:T(2,128)(2,1)S(1)}, bf16[8,2,2048]{2,1,0:T(2,128)(2,1)S(1)}, u32[]{:S(2)}, u32[]{:S(2)}) collective-permute-start(bf16[8,2,2048]{2,1,0:T(2,128)(2,1)S(1)} %get-tuple-element.36), channel_id=1, source_target_pairs={{0,1},{1,2},{2,3},{3,4},{4,5},{5,6},{6,7},{7,8},{8,9},{9,10},{10,1... | collective-permute-start | bytes 196616 | tf_op jit(solution)/shard_map/ppermute | solution.py:14
  12.4 5.6 %collective-permute-start.1 = (bf16[8,2,2048]{2,1,0:T(2,128)(2,1)S(1)}, bf16[8,2,2048]{2,1,0:T(2,128)(2,1)S(1)}, u32[]{:S(2)}, u32[]{:S(2)}) collective-permute-start(bf16[8,2,2048]{2,1,0:T(2,128)(2,1)S(1)} %get-tuple-element.37), channel_id=1, source_target_pairs={{1,0},{2,1},{3,2},{4,3},{5,4},{6,5},{7,6},{8,7},{9,8},{10,9},{11,1... | collective-permute-start | bytes 196616 | tf_op jit(solution)/shard_map/ppermute | solution.py:15
  21.2 401.4 %reduce-scatter.2.cloned.1.call-start = ((), (), s32[]{:S(2)}) async-start(), calls=%async_computation.2 | async-start | bytes 13926400 | tf_op jit(solution)/shard_map/reduce_scatter | solution.py:47
  176.6 2.1 copy-start
  236.9 9.8 %copy-start.15 = (f32[64,2048]{1,0:T(8,128)S(1)}, f32[64,2048]{1,0:T(8,128)}, u32[]{:S(2)}) copy-start(f32[64,2048]{1,0:T(8,128)} %get-tuple-element.9) | copy-start | bytes 1572868
  236.9 10.7 %copy-start.14 = (f32[64,2048]{1,0:T(8,128)S(1)}, f32[64,2048]{1,0:T(8,128)}, u32[]{:S(2)}) copy-start(f32[64,2048]{1,0:T(8,128)} %get-tuple-element.10) | copy-start | bytes 1572868
  236.9 11.5 %copy-start.8 = (f32[64,2048]{1,0:T(8,128)S(1)}, f32[64,2048]{1,0:T(8,128)}, u32[]{:S(2)}) copy-start(f32[64,2048]{1,0:T(8,128)} %get-tuple-element.32) | copy-start | bytes 1572868
  236.9 12.4 %copy-start.13 = (f32[64,2048]{1,0:T(8,128)S(1)}, f32[64,2048]{1,0:T(8,128)}, u32[]{:S(2)}) copy-start(f32[64,2048]{1,0:T(8,128)} %get-tuple-element.11) | copy-start | bytes 1572868
  236.9 13.2 %copy-start.12 = (f32[64,2048]{1,0:T(8,128)S(1)}, f32[64,2048]{1,0:T(8,128)}, u32[]{:S(2)}) copy-start(f32[64,2048]{1,0:T(8,128)} %get-tuple-element.12) | copy-start | bytes 1572868
  236.9 14.1 %copy-start.11 = (f32[64,2048]{1,0:T(8,128)S(1)}, f32[64,2048]{1,0:T(8,128)}, u32[]{:S(2)}) copy-start(f32[64,2048]{1,0:T(8,128)} %get-tuple-element.13) | copy-start | bytes 1572868
  238.9 12.9 %copy-start.7 = (f32[64,2048]{1,0:T(8,128)S(1)}, f32[64,2048]{1,0:T(8,128)}, u32[]{:S(2)}) copy-start(f32[64,2048]{1,0:T(8,128)} %get-tuple-element.16) | copy-start | bytes 1572868
  240.9 11.8 %copy-start.10 = (f32[64,2048]{1,0:T(8,128)S(1)}, f32[64,2048]{1,0:T(8,128)}, u32[]{:S(2)}) copy-start(f32[64,2048]{1,0:T(8,128)} %get-tuple-element.14) | copy-start | bytes 1572868
  242.8 10.7 %copy-start.6 = (f32[64,2048]{1,0:T(8,128)S(1)}, f32[64,2048]{1,0:T(8,128)}, u32[]{:S(2)}) copy-start(f32[64,2048]{1,0:T(8,128)} %get-tuple-element.17) | copy-start | bytes 1572868
  244.8 9.6 %copy-start.5 = (f32[64,2048]{1,0:T(8,128)S(1)}, f32[64,2048]{1,0:T(8,128)}, u32[]{:S(2)}) copy-start(f32[64,2048]{1,0:T(8,128)} %get-tuple-element.18) | copy-start | bytes 1572868
  246.7 8.5 %copy-start.4 = (f32[64,2048]{1,0:T(8,128)S(1)}, f32[64,2048]{1,0:T(8,128)}, u32[]{:S(2)}) copy-start(f32[64,2048]{1,0:T(8,128)} %get-tuple-element.19) | copy-start | bytes 1572868
  247.6 8.5 %copy-start.3 = (f32[64,2048]{1,0:T(8,128)S(1)}, f32[64,2048]{1,0:T(8,128)}, u32[]{:S(2)}) copy-start(f32[64,2048]{1,0:T(8,128)} %get-tuple-element.20) | copy-start | bytes 1572868
  248.4 8.5 %copy-start.2 = (f32[64,2048]{1,0:T(8,128)S(1)}, f32[64,2048]{1,0:T(8,128)}, u32[]{:S(2)}) copy-start(f32[64,2048]{1,0:T(8,128)} %get-tuple-element.33) | copy-start | bytes 1572868
  254.3 8.5 %copy-start.9 = (f32[64,2048]{1,0:T(8,128)S(1)}, f32[64,2048]{1,0:T(8,128)}, u32[]{:S(2)}) copy-start(f32[64,2048]{1,0:T(8,128)} %get-tuple-element.5) | copy-start | bytes 1572868
Sparse Core Ops, SparseCore 0:
  21.3 153.3 all-reduce.2
  263.9 158.7 reduce-scatter.1
where the time goes:
time: 432 us
  waiting for transfers between devices  316 us (73%)
  other arithmetic  65.3 us (15%)
  local copies, waits for them, and re-layouts  30.2 us (7%)
  between operations  13.5 us (3%)
  starting transfers between devices  6.55 us (2%)
    reduce_scatter x1, waiting for transfers between devices, body(): lax.psum_scatter(lag_products(fluctuation, rows, width), 'frame', scatter...  159 us
    psum x1, waiting for transfers between devices, body(): lax.psum(jnp.sum(raw_values, axis=0).astype(jnp.bfloat16), 'frame')  153 us
    reduce_sum x2, other arithmetic, lag_products(): products.append(jnp.sum(centre * shifted, axis=0))  58.2 us
    unnamed x56, local copies, waits for them, and re-layouts  28.1 us
  transfers between devices with their start and end apart: 4, of which 3 were waited for; matrix products, arithmetic and copies ran while one was open for 0% of the time, Pallas kernels for 0%

commit v1 on v0

--- a/solution.py
+++ b/solution.py
@@ -40,7 +40,9 @@
     padded = padded_2(movie, (("strip", 1),), 2)
     raw_values = padded.astype(jnp.float32)
     pixel_mean = (
-        lax.psum(jnp.sum(raw_values, axis=0).astype(jnp.bfloat16), "frame").astype(jnp.float32)
+        jnp.sum(
+            lax.all_gather(jnp.sum(raw_values, axis=0).astype(jnp.bfloat16), "frame"), axis=0
+        ).astype(jnp.float32)
         / frames_total
     )
     fluctuation = pad_columns(raw_values - pixel_mean)

time: 432 us -> 367 us (0.85)
  waiting for transfers between devices: 316 us -> 249 us
    psum x1 -> x0, waiting for transfers between devices: 153 us -> none  [body(): lax.psum(jnp.sum(raw_values, axis=0).astype(jnp.bfloat16), 'frame')]
    all_gather x0 -> x1, waiting for transfers between devices: none -> 87.1 us  [body(): lax.all_gather(jnp.sum(raw_values, axis=0).astype(jnp.bfloat16), 'frame')]
where the time goes in v1:
time: 367 us
  waiting for transfers between devices  249 us (68%)
  other arithmetic  67.6 us (18%)
  local copies, waits for them, and re-layouts  30.2 us (8%)
  between operations  13.5 us (4%)
  starting transfers between devices  6.55 us (2%)
    reduce_scatter x1, waiting for transfers between devices, body(): lax.psum_scatter(lag_products(fluctuation, rows, width), 'frame', scatter...  158 us
    all_gather x1, waiting for transfers between devices, body(): lax.all_gather(jnp.sum(raw_values, axis=0).astype(jnp.bfloat16), 'frame')  87.1 us
    reduce_sum x2, other arithmetic, lag_products(): products.append(jnp.sum(centre * shifted, axis=0))  58.2 us
    unnamed x56, local copies, waits for them, and re-layouts  28.1 us
  transfers between devices with their start and end apart: 4, of which 3 were waited for; matrix products, arithmetic and copies ran while one was open for 0% of the time, Pallas kernels for 0%

profile of v1, /device:TPU:1, one launch (start us, length us, event | category | flops | bytes accessed | tf_op | source)
XLA Modules:
  0.0 367.0 jit_solution(15659195387499518902)
XLA Ops:
  6.5 1.3 fusion.5
  7.8 4.6 %collective-permute-start = (bf16[8,2,2048]{2,1,0:T(2,128)(2,1)S(1)}, bf16[8,2,2048]{2,1,0:T(2,128)(2,1)S(1)}, u32[]{:S(2)}, u32[]{:S(2)}) collective-permute-start(bf16[8,2,2048]{2,1,0:T(2,128)(2,1)S(1)} %get-tuple-element.36), channel_id=1, source_target_pairs={{0,1},{1,2},{2,3},{3,4},{4,5},{5,6},{6,7},{7,8},{8,9},{9,10},{10,1... | collective-permute-start | bytes 196616 | tf_op jit(solution)/shard_map/ppermute | solution.py:14
  12.4 1.9 collective-permute-start.1
  14.4 3.6 collective-permute-done.1
  18.0 3.1 fusion.4
  21.2 87.1 %all-gather.4.cloned.1.call-done = bf16[16,68,2048]{2,1,0:T(8,128)(2,1)} async-done(((bf16[1,68,2048]{2,1,0:T(8,128)(2,1)}), bf16[16,68,2048]{2,1,0:T(8,128)(2,1)}) %all-gather.4.cloned.1.call-update) | async-done | bytes 4456464 | tf_op jit(solution)/shard_map/all_gather | solution.py:44
  108.3 3.3 reduce_sum.250
  111.6 0.9 convert_subtract_fusion
  112.5 2.1 copy-done
  114.6 13.1 %multiply_reduce_fusion = (f32[64,2048]{1,0:T(8,128)}, f32[64,2048]{1,0:T(8,128)}, f32[64,2048]{1,0:T(8,128)}, f32[64,2048]{1,0:T(8,128)}, f32[64,2048]{1,0:T(8,...) fusion(f32[8,68,2048]{2,1,0:T(8,128)S(1)} %convert_subtract_fusion), kind=kLoop, calls=%fused_computation.9 | loop fusion | flops 19660800 | bytes 14155776 | tf_op jit(solution)/shard_map/reduce_sum | solution.py:28
  127.7 45.1 %multiply_reduce_fusion.1 = (f32[64,2048]{1,0:T(8,128)S(1)}, f32[64,2048]{1,0:T(8,128)}, f32[64,2048]{1,0:T(8,128)}, f32[64,2048]{1,0:T(8,128)}, f32[64,2048]{1,...) fusion(f32[8,68,2048]{2,1,0:T(8,128)} %copy-done), kind=kLoop, calls=%fused_computation.10 | loop fusion | flops 29491200 | bytes 33554432 | tf_op jit(solution)/shard_map/reduce_sum | solution.py:28
  172.8 2.0 bitcast_dynamic-update-slice_fusion.24
  174.9 1.9 bitcast_dynamic-update-slice_fusion.23
  176.8 2.0 bitcast_dynamic-update-slice_fusion.22
  178.8 1.9 bitcast_dynamic-update-slice_fusion.21
  180.7 1.9 bitcast_dynamic-update-slice_fusion.20
  182.7 0.8 bitcast_dynamic-update-slice_fusion.19
  184.3 0.8 bitcast_dynamic-update-slice_fusion.17
  186.0 0.9 bitcast_dynamic-update-slice_fusion.15
  186.9 0.8 bitcast_dynamic-update-slice_fusion.14
  187.7 0.8 bitcast_dynamic-update-slice_fusion.13
  188.6 0.8 bitcast_dynamic-update-slice_fusion.12
  189.4 0.9 bitcast_dynamic-update-slice_fusion.11
  191.1 0.8 bitcast_dynamic-update-slice_fusion.9
  192.0 0.9 bitcast_dynamic-update-slice_fusion.8
  192.8 0.9 bitcast_dynamic-update-slice_fusion.7
  195.4 0.9 bitcast_dynamic-update-slice_fusion.4
  196.3 0.8 bitcast_dynamic-update-slice_fusion.3
  197.9 0.8 bitcast_dynamic-update-slice_fusion.1
  198.8 0.9 bitcast_dynamic-update-slice_fusion
  199.7 158.4 %reduce-scatter.2.cloned.1.call-done = f32[25,64,128]{2,1,0:T(8,128)} async-done(((f32[25,64,2048]{2,1,0:T(8,128)}), f32[25,64,128]{2,1,0:T(8,128)}) %reduce-scatter.2.cloned.1.call-update) | async-done | bytes 819216 | tf_op jit(solution)/shard_map/reduce_scatter | solution.py:49
  358.1 2.1 broadcast_multiply_fusion
  (43 shorter events, 5.1 us)
Async XLA Ops:
  6.5 105.1 %copy-start.1 = (bf16[8,64,2048]{2,1,0:T(8,128)(2,1)S(1)}, bf16[8,64,2048]{2,1,0:T(8,128)(2,1)}, u32[]{:S(2)}) copy-start(bf16[8,64,2048]{2,1,0:T(8,128)(2,1)} %param.1) | copy-start | bytes 6291460
  6.5 101.7 %all-gather.4.cloned.1.call-start = ((), (), s32[]{:S(2)}) async-start(), calls=%async_computation.2 | async-start | bytes 5013504 | tf_op jit(solution)/shard_map/all_gather | solution.py:44
  7.8 6.5 %collective-permute-start = (bf16[8,2,2048]{2,1,0:T(2,128)(2,1)S(1)}, bf16[8,2,2048]{2,1,0:T(2,128)(2,1)S(1)}, u32[]{:S(2)}, u32[]{:S(2)}) collective-permute-start(bf16[8,2,2048]{2,1,0:T(2,128)(2,1)S(1)} %get-tuple-element.36), channel_id=1, source_target_pairs={{0,1},{1,2},{2,3},{3,4},{4,5},{5,6},{6,7},{7,8},{8,9},{9,10},{10,1... | collective-permute-start | bytes 196616 | tf_op jit(solution)/shard_map/ppermute | solution.py:14
  12.4 5.6 %collective-permute-start.1 = (bf16[8,2,2048]{2,1,0:T(2,128)(2,1)S(1)}, bf16[8,2,2048]{2,1,0:T(2,128)(2,1)S(1)}, u32[]{:S(2)}, u32[]{:S(2)}) collective-permute-start(bf16[8,2,2048]{2,1,0:T(2,128)(2,1)S(1)} %get-tuple-element.37), channel_id=1, source_target_pairs={{1,0},{2,1},{3,2},{4,3},{5,4},{6,5},{7,6},{8,7},{9,8},{10,9},{11,1... | collective-permute-start | bytes 196616 | tf_op jit(solution)/shard_map/ppermute | solution.py:15
  21.2 336.9 %reduce-scatter.2.cloned.1.call-start = ((), (), s32[]{:S(2)}) async-start(), calls=%async_computation.1 | async-start | bytes 13926400 | tf_op jit(solution)/shard_map/reduce_scatter | solution.py:49
  112.5 2.1 copy-start
  172.8 9.8 %copy-start.15 = (f32[64,2048]{1,0:T(8,128)S(1)}, f32[64,2048]{1,0:T(8,128)}, u32[]{:S(2)}) copy-start(f32[64,2048]{1,0:T(8,128)} %get-tuple-element.9) | copy-start | bytes 1572868
  172.8 10.7 %copy-start.14 = (f32[64,2048]{1,0:T(8,128)S(1)}, f32[64,2048]{1,0:T(8,128)}, u32[]{:S(2)}) copy-start(f32[64,2048]{1,0:T(8,128)} %get-tuple-element.10) | copy-start | bytes 1572868
  172.8 11.5 %copy-start.8 = (f32[64,2048]{1,0:T(8,128)S(1)}, f32[64,2048]{1,0:T(8,128)}, u32[]{:S(2)}) copy-start(f32[64,2048]{1,0:T(8,128)} %get-tuple-element.32) | copy-start | bytes 1572868
  172.8 12.4 %copy-start.13 = (f32[64,2048]{1,0:T(8,128)S(1)}, f32[64,2048]{1,0:T(8,128)}, u32[]{:S(2)}) copy-start(f32[64,2048]{1,0:T(8,128)} %get-tuple-element.11) | copy-start | bytes 1572868
  172.8 13.2 %copy-start.12 = (f32[64,2048]{1,0:T(8,128)S(1)}, f32[64,2048]{1,0:T(8,128)}, u32[]{:S(2)}) copy-start(f32[64,2048]{1,0:T(8,128)} %get-tuple-element.12) | copy-start | bytes 1572868
  172.8 14.1 %copy-start.11 = (f32[64,2048]{1,0:T(8,128)S(1)}, f32[64,2048]{1,0:T(8,128)}, u32[]{:S(2)}) copy-start(f32[64,2048]{1,0:T(8,128)} %get-tuple-element.13) | copy-start | bytes 1572868
  174.9 12.9 %copy-start.7 = (f32[64,2048]{1,0:T(8,128)S(1)}, f32[64,2048]{1,0:T(8,128)}, u32[]{:S(2)}) copy-start(f32[64,2048]{1,0:T(8,128)} %get-tuple-element.16) | copy-start | bytes 1572868
  176.8 11.8 %copy-start.10 = (f32[64,2048]{1,0:T(8,128)S(1)}, f32[64,2048]{1,0:T(8,128)}, u32[]{:S(2)}) copy-start(f32[64,2048]{1,0:T(8,128)} %get-tuple-element.14) | copy-start | bytes 1572868
  178.8 10.7 %copy-start.6 = (f32[64,2048]{1,0:T(8,128)S(1)}, f32[64,2048]{1,0:T(8,128)}, u32[]{:S(2)}) copy-start(f32[64,2048]{1,0:T(8,128)} %get-tuple-element.17) | copy-start | bytes 1572868
  180.7 9.6 %copy-start.5 = (f32[64,2048]{1,0:T(8,128)S(1)}, f32[64,2048]{1,0:T(8,128)}, u32[]{:S(2)}) copy-start(f32[64,2048]{1,0:T(8,128)} %get-tuple-element.18) | copy-start | bytes 1572868
  182.6 8.5 %copy-start.4 = (f32[64,2048]{1,0:T(8,128)S(1)}, f32[64,2048]{1,0:T(8,128)}, u32[]{:S(2)}) copy-start(f32[64,2048]{1,0:T(8,128)} %get-tuple-element.19) | copy-start | bytes 1572868
  183.5 8.5 %copy-start.3 = (f32[64,2048]{1,0:T(8,128)S(1)}, f32[64,2048]{1,0:T(8,128)}, u32[]{:S(2)}) copy-start(f32[64,2048]{1,0:T(8,128)} %get-tuple-element.20) | copy-start | bytes 1572868
  184.3 8.5 %copy-start.2 = (f32[64,2048]{1,0:T(8,128)S(1)}, f32[64,2048]{1,0:T(8,128)}, u32[]{:S(2)}) copy-start(f32[64,2048]{1,0:T(8,128)} %get-tuple-element.33) | copy-start | bytes 1572868
  190.3 8.5 %copy-start.9 = (f32[64,2048]{1,0:T(8,128)S(1)}, f32[64,2048]{1,0:T(8,128)}, u32[]{:S(2)}) copy-start(f32[64,2048]{1,0:T(8,128)} %get-tuple-element.5) | copy-start | bytes 1572868
Sparse Core Ops, SparseCore 0:
  21.3 86.9 all-gather.3
  199.8 158.2 reduce-scatter.1
